TPU v7x, 32 devices: a whole 2x2x4 slice. The times are simulated.
32 devices in a mesh: seq: 2 (over x), batch: 4 (over y, core), head: 4 (over z).
Axes of the slice: x: 2, y: 2, z: 4, core: 2. Of those that a mesh axis runs over, the one named last changes fastest.
Arguments:
- hidden: bfloat16 [4, 256, 16384], P('batch', None, 'seq'), may hold values from -760 to 760
- gain: float32 [16384], P('seq'), may hold values from 0.5 to 1.5
- key_weight: bfloat16 [16384, 1024], P('seq', 'head'), may hold values from -0.046875 to 0.046875
- value_weight: bfloat16 [16384, 1024], P('seq', 'head'), may hold values from -0.046875 to 0.046875
- positions: int32 [4, 256], P('batch', 'seq'), may hold values from 0 to 32767
- initial_basis: float32 [2048, 256], P('head'), may hold values from -6 to 6
Outputs:
- basis: float32 [2048, 256], P('head')
All inputs are finite; a program needn't handle non-finite values.
Results may differ from a plain program's by a relative error of at most 0.0063.
Values may be sent and summed in bfloat16 or wider, within the bound.
A program may use at most 64 MiB of HBM per device.

v0:
```python
import math
import jax
import jax.numpy as jnp
from jax import lax
from jax.sharding import PartitionSpec as P

D = 16384
HEAD_DIM = 128
ITERS = 4
EPSILON = 1e-05
ROTARY_BASE = 500000.0


def rotary(head_rows, position_row):
    half_width = head_rows.shape[-1] // 2
    index_row = jnp.arange(half_width, dtype=jnp.float32)
    frequency = jnp.exp(index_row * (-math.log(ROTARY_BASE) / half_width))
    angles = position_row.astype(jnp.float32)[:, None] * frequency[None, :]
    cosine = jnp.cos(angles)[:, None, :]
    sine_part = jnp.sin(angles)[:, None, :]
    first_half = head_rows[..., :half_width]
    second_half = head_rows[..., half_width:]
    return jnp.concatenate(
        [
            first_half * cosine - second_half * sine_part,
            second_half * cosine + first_half * sine_part,
        ],
        axis=-1,
    )


def whole_of(basis_block):
    return lax.all_gather(basis_block, "head", axis=0, tiled=True)


def total_squares(local_squares, local_tokens):
    all_squares = lax.psum(local_squares, "seq")
    return lax.dynamic_slice_in_dim(all_squares, lax.axis_index("seq") * local_tokens, local_tokens)


def gram_of(images):
    return lax.dot_general(
        images,
        images,
        (((0,), (0,)), ((), ())),
        precision=lax.Precision.HIGHEST,
        preferred_element_type=jnp.float32,
    )


def orthonormal(images, gram_matrix):
    factor = jnp.linalg.cholesky(gram_matrix)
    return lax.linalg.triangular_solve(
        factor, images, left_side=False, lower=True, transpose_a=True
    )


def body(hidden, gain, key_weight, value_weight, positions, initial_basis):
    hidden_rows = hidden[0]
    local_tokens = positions.shape[1]
    widened = hidden_rows.astype(jnp.float32)
    scaled = (widened * gain).astype(jnp.bfloat16)
    local_squares = jnp.sum(widened * widened, axis=1)
    key_columns = key_weight.shape[1]
    weights = jnp.concatenate([key_weight, value_weight], axis=1)
    own_squares = total_squares(local_squares, local_tokens)
    projected = lax.psum_scatter(
        jnp.dot(scaled, weights, preferred_element_type=jnp.float32),
        "seq",
        scatter_dimension=0,
        tiled=True,
    )
    inverse_scale = lax.rsqrt(own_squares / D + EPSILON)
    projected = projected * inverse_scale[:, None]
    key_rows = rotary(projected[:, :key_columns].reshape(local_tokens, -1, HEAD_DIM), positions[0])
    value_rows = projected[:, key_columns:].reshape(local_tokens, -1, HEAD_DIM)
    joint_rows = (
        jnp.stack([key_rows, value_rows], axis=2).reshape(local_tokens, -1).astype(jnp.bfloat16)
    )
    partial_value = lax.dot_general(
        joint_rows,
        lax.all_gather(joint_rows, "head", axis=1, tiled=True),
        (((0,), (0,)), ((), ())),
        preferred_element_type=jnp.float32,
    )
    token_total = local_tokens * lax.axis_size("seq") * lax.axis_size("batch")
    basis_block = initial_basis
    covariance = lax.psum(partial_value, ("seq", "batch")) / token_total
    for iteration in range(ITERS):
        whole_basis = whole_of(basis_block)
        images = jnp.dot(
            covariance,
            whole_basis,
            precision=lax.Precision.HIGHEST,
            preferred_element_type=jnp.float32,
        )
        gram_matrix = lax.psum(gram_of(images), "head") / whole_basis.shape[0]
        basis_block = orthonormal(images, gram_matrix)
    return basis_block


def solution(mesh):
    return jax.shard_map(
        body,
        mesh=mesh,
        in_specs=(
            P("batch", None, "seq"),
            P("seq"),
            P("seq", "head"),
            P("seq", "head"),
            P("batch", "seq"),
            P("head", None),
        ),
        out_specs=P("head", None),
        check_vma=False,
    )
```

profile of v0, /device:TPU:0, one launch (start us, length us, event | category | flops | bytes accessed | tf_op | source)
XLA Modules:
  0.0 718.3 jit_solution(16877559719014018275)
XLA Ops:
  7.4 7.8 %fusion.2 = f32[256,512]{1,0:T(8,128)} fusion(bf16[8192,256]{1,0:T(8,128)(2,1)} %param.12, bf16[8192,256]{1,0:T(8,128)(2,1)} %param.11, bf16[1,256,8192]{2,1,0:T(8,128)(2,1)} %param.9, f32[8192]{0:T(1024)} %param.10), kind=kOutput, calls=%fused_computation.12 | convolution fusion | flops 2170552320 | bytes 13139968 | tf_op jit(solution)/shard_map/dot_general | solution.py:68
  15.2 3.1 fusion.1
  18.4 5.9 psum.42
  24.5 8.2 %reduce-scatter.2.cloned.1.call-done = f32[128,512]{1,0:T(8,128)} async-done(((f32[256,512]{1,0:T(8,128)}), f32[128,512]{1,0:T(8,128)}) %reduce-scatter.2.cloned.1.call-update) | async-done | bytes 262160 | tf_op jit(solution)/shard_map/reduce_scatter | solution.py:67
  34.1 15.5 %all_gather.15 = bf16[128,2048]{0,1:T(8,128)(2,1)S(1)} all-gather(bf16[128,512]{0,1:T(8,128)(2,1)S(1)} %bitcast.160), channel_id=1, replica_groups=mesh['seq'=2,'batch'=4,'head'=4] {'head'}, dimensions={1}, use_global_device_ids=true | all-gather | bytes 655360 | tf_op jit(solution)/shard_map/all_gather | solution.py:82
  49.6 2.7 fusion.74
  52.9 81.2 %all-reduce.7.cloned.1.call-done = f32[512,2048]{1,0:T(8,128)} async-done(((f32[512,2048]{1,0:T(8,128)}), f32[512,2048]{1,0:T(8,128)}) %all-reduce.7.cloned.1.call-update) | async-done | bytes 4194320 | tf_op jit(solution)/shard_map/psum | solution.py:88
  134.1 6.1 fusion.15
  140.2 1.7 fusion.75
  142.3 35.4 %all-reduce.9.cloned.1.call-done = f32[256,256]{0,1:T(8,128)} async-done(((f32[256,256]{0,1:T(8,128)}), f32[256,256]{0,1:T(8,128)}) %all-reduce.9.cloned.1.call-update) | async-done | bytes 262160 | tf_op jit(solution)/shard_map/psum | solution.py:97
  179.8 11.7 %cholesky.214 = f32[128,128]{1,0:T(8,128)S(1)} custom-call(f32[128,128]{1,0:T(8,128)S(1)} %cholesky.346), custom_call_target="Cholesky" | custom-call | tf_op jit(solution)/shard_map/jit(cholesky)/cholesky | solution.py:52
  191.5 9.8 %custom-call.17 = f32[1,128,128]{1,2,0:T(8,128)S(1)} custom-call(f32[1,128,128]{2,1,0:T(8,128)S(1)} %get-tuple-element.94), custom_call_target="InvertDiagBlocksLowerTriangular" | custom-call | tf_op jit(solution)/shard_map/jit(cholesky)/cholesky | solution.py:52
  201.8 11.7 %cholesky.231 = f32[128,128]{1,0:T(8,128)S(1)} custom-call(f32[128,128]{1,0:T(8,128)S(1)} %convolution_subtract_fusion.7), custom_call_target="Cholesky" | custom-call | tf_op jit(solution)/shard_map/jit(cholesky)/cholesky | solution.py:52
  215.6 4.5 while.8
  216.8 1.4 bitcast_dynamic-update-slice_fusion.8
  218.7 1.4 bitcast_dynamic-update-slice_fusion.8
  220.1 19.7 %custom-call.18 = f32[2,128,128]{1,2,0:T(8,128)S(1)} custom-call(f32[2,128,128]{2,1,0:T(8,128)S(1)} %get-tuple-element.33), custom_call_target="InvertDiagBlocksLowerTriangular" | custom-call | tf_op jit(solution)/shard_map/triangular_solve/custom-call.0 | solution.py:53
  242.1 45.1 %all-gather.7.cloned.1.call-done = f32[2048,256]{0,1:T(8,128)} async-done(((f32[512,256]{0,1:T(8,128)}), f32[2048,256]{0,1:T(8,128)}) %all-gather.7.cloned.1.call-update) | async-done | bytes 2097168 | tf_op jit(solution)/shard_map/all_gather | solution.py:33
  287.2 6.1 fusion.13
  293.3 1.7 fusion.76
  295.3 34.3 %all-reduce.11.cloned.1.call-done = f32[256,256]{0,1:T(8,128)} async-done(((f32[256,256]{0,1:T(8,128)}), f32[256,256]{0,1:T(8,128)}) %all-reduce.11.cloned.1.call-update) | async-done | bytes 262160 | tf_op jit(solution)/shard_map/psum | solution.py:97
  331.6 11.7 %cholesky.248 = f32[128,128]{1,0:T(8,128)S(1)} custom-call(f32[128,128]{1,0:T(8,128)S(1)} %cholesky.349), custom_call_target="Cholesky" | custom-call | tf_op jit(solution)/shard_map/jit(cholesky)/cholesky | solution.py:52
  343.4 9.8 %custom-call.19 = f32[1,128,128]{1,2,0:T(8,128)S(1)} custom-call(f32[1,128,128]{2,1,0:T(8,128)S(1)} %get-tuple-element.90), custom_call_target="InvertDiagBlocksLowerTriangular" | custom-call | tf_op jit(solution)/shard_map/jit(cholesky)/cholesky | solution.py:52
  353.7 11.7 %cholesky.265 = f32[128,128]{1,0:T(8,128)S(1)} custom-call(f32[128,128]{1,0:T(8,128)S(1)} %convolution_subtract_fusion.6), custom_call_target="Cholesky" | custom-call | tf_op jit(solution)/shard_map/jit(cholesky)/cholesky | solution.py:52
  368.1 4.2 while.9
  368.9 1.4 bitcast_dynamic-update-slice_fusion.9
  370.9 1.4 bitcast_dynamic-update-slice_fusion.9
  372.2 19.7 %custom-call.20 = f32[2,128,128]{1,2,0:T(8,128)S(1)} custom-call(f32[2,128,128]{2,1,0:T(8,128)S(1)} %get-tuple-element.34), custom_call_target="InvertDiagBlocksLowerTriangular" | custom-call | tf_op jit(solution)/shard_map/triangular_solve/custom-call.0 | solution.py:53
  394.3 45.1 %all-gather.9.cloned.1.call-done = f32[2048,256]{0,1:T(8,128)} async-done(((f32[512,256]{0,1:T(8,128)}), f32[2048,256]{0,1:T(8,128)}) %all-gather.9.cloned.1.call-update) | async-done | bytes 2097168 | tf_op jit(solution)/shard_map/all_gather | solution.py:33
  439.4 6.1 fusion.11
  445.4 1.7 fusion.77
  447.5 34.1 %all-reduce.13.cloned.1.call-done = f32[256,256]{0,1:T(8,128)} async-done(((f32[256,256]{0,1:T(8,128)}), f32[256,256]{0,1:T(8,128)}) %all-reduce.13.cloned.1.call-update) | async-done | bytes 262160 | tf_op jit(solution)/shard_map/psum | solution.py:97
  483.7 11.7 %cholesky.282 = f32[128,128]{1,0:T(8,128)S(1)} custom-call(f32[128,128]{1,0:T(8,128)S(1)} %cholesky.352), custom_call_target="Cholesky" | custom-call | tf_op jit(solution)/shard_map/jit(cholesky)/cholesky | solution.py:52
  495.5 9.8 %custom-call.21 = f32[1,128,128]{1,2,0:T(8,128)S(1)} custom-call(f32[1,128,128]{2,1,0:T(8,128)S(1)} %get-tuple-element.86), custom_call_target="InvertDiagBlocksLowerTriangular" | custom-call | tf_op jit(solution)/shard_map/jit(cholesky)/cholesky | solution.py:52
  505.8 11.7 %cholesky.299 = f32[128,128]{1,0:T(8,128)S(1)} custom-call(f32[128,128]{1,0:T(8,128)S(1)} %convolution_subtract_fusion.5), custom_call_target="Cholesky" | custom-call | tf_op jit(solution)/shard_map/jit(cholesky)/cholesky | solution.py:52
  520.2 15.9 %while.10 = (s32[]{:T(128)}, f32[256,256]{1,0:T(8,128)S(1)}, s32[2,2]{1,0:T(2,128)S(1)}, f32[2,128,128]{2,1,0:T(8,128)S(1)}, s32[]{:T(128)}) while((s32[]{:T(128)}, f32[256,256]{1,0:T(8,128)S(1)}, s32[2,2]{1,0:T(2,128)S(1)}, f32[2,128,128]{2,1,0:T(8,128)S(1)}, s32[]{:T(128)}) %tuple.112), condition=%wide.while_cond.clone.1, body=%wide.while_body.clone.1.sunk | while | flops 2 | bytes 131181 | solution.py:53
  536.1 19.7 %custom-call.22 = f32[2,128,128]{1,2,0:T(8,128)S(1)} custom-call(f32[2,128,128]{2,1,0:T(8,128)S(1)} %get-tuple-element.35), custom_call_target="InvertDiagBlocksLowerTriangular" | custom-call | tf_op jit(solution)/shard_map/triangular_solve/custom-call.0 | solution.py:53
  558.1 45.1 %all-gather.11.cloned.1.call-done = f32[2048,256]{0,1:T(8,128)} async-done(((f32[512,256]{0,1:T(8,128)}), f32[2048,256]{0,1:T(8,128)}) %all-gather.11.cloned.1.call-update) | async-done | bytes 2097168 | tf_op jit(solution)/shard_map/all_gather | solution.py:33
  603.2 6.1 fusion.9
  609.3 1.7 fusion.78
  611.0 34.5 %all-reduce.15.cloned.1.call-done = f32[256,256]{0,1:T(8,128)} async-done(((f32[256,256]{0,1:T(8,128)}), f32[256,256]{0,1:T(8,128)}) %all-reduce.15.cloned.1.call-update) | async-done | bytes 262160 | tf_op jit(solution)/shard_map/psum | solution.py:97
  647.6 11.7 %cholesky.316 = f32[128,128]{1,0:T(8,128)S(1)} custom-call(f32[128,128]{1,0:T(8,128)S(1)} %cholesky.355), custom_call_target="Cholesky" | custom-call | tf_op jit(solution)/shard_map/jit(cholesky)/cholesky | solution.py:52
  659.4 9.8 %custom-call.23 = f32[1,128,128]{1,2,0:T(8,128)S(1)} custom-call(f32[1,128,128]{2,1,0:T(8,128)S(1)} %get-tuple-element.82), custom_call_target="InvertDiagBlocksLowerTriangular" | custom-call | tf_op jit(solution)/shard_map/jit(cholesky)/cholesky | solution.py:52
  669.7 11.7 %cholesky.333 = f32[128,128]{1,0:T(8,128)S(1)} custom-call(f32[128,128]{1,0:T(8,128)S(1)} %convolution_subtract_fusion.4), custom_call_target="Cholesky" | custom-call | tf_op jit(solution)/shard_map/jit(cholesky)/cholesky | solution.py:52
  684.2 4.1 while.11
  684.8 1.4 bitcast_dynamic-update-slice_fusion.11
  686.8 1.4 bitcast_dynamic-update-slice_fusion.11
  688.3 19.9 %custom-call.24 = f32[2,128,128]{1,2,0:T(8,128)S(1)} custom-call(f32[2,128,128]{2,1,0:T(8,128)S(1)} %get-tuple-element.36), custom_call_target="InvertDiagBlocksLowerTriangular" | custom-call | tf_op jit(solution)/shard_map/triangular_solve/custom-call.0 | solution.py:53
  (123 shorter events, 35.5 us)
Async XLA Ops:
  7.4 25.3 %reduce-scatter.2.cloned.1.call-start = ((), (), s32[]{:S(2)}) async-start(), calls=%async_computation.1 | async-start | bytes 786432 | tf_op jit(solution)/shard_map/reduce_scatter | solution.py:67
  15.2 9.1 %copy-start = (s32[1,128]{1,0:T(1,128)S(1)}, s32[1,128]{1,0:T(1,128)}, u32[]{:S(2)}) copy-start(s32[1,128]{1,0:T(1,128)} %param.13) | copy-start | bytes 1540
  15.2 118.9 %all-reduce.7.cloned.1.call-start = ((), (), s32[]{:S(2)}) async-start(), calls=%async_computation.2 | async-start | bytes 8388608 | tf_op jit(solution)/shard_map/psum | solution.py:88
  52.3 81.8 %all-gather.5.cloned.1.call-start = ((), (), s32[]{:S(2)}) async-start(), calls=%async_computation.3 | async-start | bytes 2621440 | tf_op jit(solution)/shard_map/all_gather | solution.py:33
  52.9 124.8 %all-reduce.9.cloned.1.call-start = ((), (), s32[]{:S(2)}) async-start(), calls=%async_computation.4 | async-start | bytes 524288 | tf_op jit(solution)/shard_map/psum | solution.py:97
  141.9 145.3 %all-gather.7.cloned.1.call-start = ((), (), s32[]{:S(2)}) async-start(), calls=%async_computation.5 | async-start | bytes 2621440 | tf_op jit(solution)/shard_map/all_gather | solution.py:33
  242.1 87.4 %all-reduce.11.cloned.1.call-start = ((), (), s32[]{:S(2)}) async-start(), calls=%async_computation.6 | async-start | bytes 524288 | tf_op jit(solution)/shard_map/psum | solution.py:97
  295.0 144.3 %all-gather.9.cloned.1.call-start = ((), (), s32[]{:S(2)}) async-start(), calls=%async_computation.7 | async-start | bytes 2621440 | tf_op jit(solution)/shard_map/all_gather | solution.py:33
  394.2 87.4 %all-reduce.13.cloned.1.call-start = ((), (), s32[]{:S(2)}) async-start(), calls=%async_computation.8 | async-start | bytes 524288 | tf_op jit(solution)/shard_map/psum | solution.py:97
  447.2 156.0 %all-gather.11.cloned.1.call-start = ((), (), s32[]{:S(2)}) async-start(), calls=%async_computation.9 | async-start | bytes 2621440 | tf_op jit(solution)/shard_map/all_gather | solution.py:33
  558.0 87.4 %all-reduce.15.cloned.1.call-start = ((), (), s32[]{:S(2)}) async-start(), calls=%async_computation.10 | async-start | bytes 524288 | tf_op jit(solution)/shard_map/psum | solution.py:97
Sparse Core Ops, SparseCore 0:
  15.3 17.3 reduce-scatter.1
  52.4 81.6 all-reduce.6
Sparse Core Ops, SparseCore 1:
  54.3 46.3 all-gather.4
  142.0 35.6 all-reduce.8
  242.2 45.0 all-gather.6
  295.1 34.3 all-reduce.10
  394.3 45.0 all-gather.8
  447.3 34.3 all-reduce.12
  558.1 45.0 all-gather.10
  611.1 34.3 all-reduce.14
where the time goes:
time: 725 us; the launch traced here: 718 us
  waiting for transfers between devices  364 us (50%)
  other arithmetic  232 us (32%)
  matrix products  49.2 us (7%)
  blocking collectives  21.4 us (3%)
  between operations  20.9 us (3%)
  local copies, waits for them, and re-layouts  17.7 us (2%)
  loops' own time  12.9 us (2%)
    psum x4, waiting for transfers between devices, body(): gram_matrix = lax.psum(gram_of(images), 'head') / whole_basis.shape[0]  138 us
    another operation x27, other arithmetic, orthonormal(): factor = jnp.linalg.cholesky(gram_matrix)  138 us
    all_gather x4, waiting for transfers between devices, whole_of(): return lax.all_gather(basis_block, 'head', axis=0, tiled=True)  135 us
    another operation x13, other arithmetic, orthonormal(): lax.linalg.triangular_solve(factor, images, left_side=False, lower=True,...  81.6 us
    psum x1, waiting for transfers between devices, body(): covariance = lax.psum(partial_value, ('seq', 'batch')) / token_total  81.2 us
    dot_general x4, matrix products, body(): jnp.dot(covariance, whole_basis, precision=lax.Precision.HIGHEST, preferr...  24.3 us
    another operation x30, local copies, waits for them, and re-layouts, orthonormal(): lax.linalg.triangular_solve(factor, images, left_side=False, lower=True,...  16.8 us
    all_gather x1, blocking collectives, body(): lax.all_gather(joint_rows, 'head', axis=1, tiled=True)  15.5 us
  transfers between devices with their start and end apart: 10, of which 9 were waited for; matrix products, arithmetic and copies ran while one was open for 0% of the time, Pallas kernels for 0%

commit v1 on v0

--- a/solution.py
+++ b/solution.py
@@ -85,7 +85,7 @@
     )
     token_total = local_tokens * lax.axis_size("seq") * lax.axis_size("batch")
     basis_block = initial_basis
-    covariance = lax.psum(partial_value, ("seq", "batch")) / token_total
+    covariance = lax.psum(lax.psum(partial_value, "batch"), "seq") / token_total
     for iteration in range(ITERS):
         whole_basis = whole_of(basis_block)
         images = jnp.dot(

time: 725 us -> 839 us (1.16)
  waiting for transfers between devices: 364 us -> 479 us
    psum x1 -> x2, waiting for transfers between devices: 81.2 us -> 196 us  [body(): covariance = lax.psum(lax.psum(partial_value, 'batch'), 'seq') / token_total]
  transfers between devices with their start and end apart: 10 -> 11, of which waited for: 9 -> 10; matrix products, arithmetic and copies ran while one was open for 0% -> 0% of each run, Pallas kernels for 0% -> 0%
where the time goes in v1:
time: 839 us; the launch traced here: 833 us
  waiting for transfers between devices  479 us (57%)
  other arithmetic  232 us (28%)
  matrix products  49.1 us (6%)
  blocking collectives  21.4 us (3%)
  between operations  20.6 us (2%)
  local copies, waits for them, and re-layouts  17.7 us (2%)
  loops' own time  12.9 us (2%)
    psum x2, waiting for transfers between devices, body(): covariance = lax.psum(lax.psum(partial_value, 'batch'), 'seq') / token_total  196 us
    psum x4, waiting for transfers between devices, body(): gram_matrix = lax.psum(gram_of(images), 'head') / whole_basis.shape[0]  138 us
    another operation x27, other arithmetic, orthonormal(): factor = jnp.linalg.cholesky(gram_matrix)  138 us
    all_gather x4, waiting for transfers between devices, whole_of(): return lax.all_gather(basis_block, 'head', axis=0, tiled=True)  135 us
    another operation x13, other arithmetic, orthonormal(): lax.linalg.triangular_solve(factor, images, left_side=False, lower=True,...  81.6 us
    dot_general x4, matrix products, body(): jnp.dot(covariance, whole_basis, precision=lax.Precision.HIGHEST, preferr...  24.3 us
    another operation x30, local copies, waits for them, and re-layouts, orthonormal(): lax.linalg.triangular_solve(factor, images, left_side=False, lower=True,...  16.8 us
  transfers between devices with their start and end apart: 11, of which 10 were waited for; matrix products, arithmetic and copies ran while one was open for 0% of the time, Pallas kernels for 0%

profile of v1, /device:TPU:0, one launch (start us, length us, event | category | flops | bytes accessed | tf_op | source)
XLA Modules:
  0.0 833.1 jit_solution(3968858663092362732)
XLA Ops:
  7.4 7.8 fusion.2
  15.2 3.1 fusion.1
  18.4 5.9 psum.49
  24.5 8.2 reduce-scatter.2.cloned.1.call-done
  34.1 15.5 %all_gather.15 = bf16[128,2048]{0,1:T(8,128)(2,1)S(1)} all-gather(bf16[128,512]{0,1:T(8,128)(2,1)S(1)} %bitcast.160), channel_id=1, replica_groups=mesh['seq'=2,'batch'=4,'head'=4] {'head'}, dimensions={1}, use_global_device_ids=true | all-gather | bytes 655360 | tf_op jit(solution)/shard_map/all_gather | solution.py:82
  49.6 2.6 fusion.74
  52.9 85.8 %all-reduce.8.cloned.1.call-done = f32[512,2048]{1,0:T(8,128)} async-done(((f32[512,2048]{1,0:T(8,128)}), f32[512,2048]{1,0:T(8,128)}) %all-reduce.8.cloned.1.call-update) | async-done | bytes 4194320 | tf_op jit(solution)/shard_map/psum | solution.py:88
  138.8 110.4 %all-reduce.10.cloned.1.call-done = f32[512,2048]{1,0:T(8,128)} async-done(((f32[512,2048]{1,0:T(8,128)}), f32[512,2048]{1,0:T(8,128)}) %all-reduce.10.cloned.1.call-update) | async-done | bytes 4194320 | tf_op jit(solution)/shard_map/psum | solution.py:88
  249.2 6.1 fusion.15
  255.3 1.7 fusion.75
  257.4 35.3 %all-reduce.12.cloned.1.call-done = f32[256,256]{0,1:T(8,128)} async-done(((f32[256,256]{0,1:T(8,128)}), f32[256,256]{0,1:T(8,128)}) %all-reduce.12.cloned.1.call-update) | async-done | bytes 262160 | tf_op jit(solution)/shard_map/psum | solution.py:97
  294.9 11.7 %cholesky.214 = f32[128,128]{1,0:T(8,128)S(1)} custom-call(f32[128,128]{1,0:T(8,128)S(1)} %cholesky.346), custom_call_target="Cholesky" | custom-call | tf_op jit(solution)/shard_map/jit(cholesky)/cholesky | solution.py:52
  306.6 9.8 %custom-call.17 = f32[1,128,128]{1,2,0:T(8,128)S(1)} custom-call(f32[1,128,128]{2,1,0:T(8,128)S(1)} %get-tuple-element.94), custom_call_target="InvertDiagBlocksLowerTriangular" | custom-call | tf_op jit(solution)/shard_map/jit(cholesky)/cholesky | solution.py:52
  316.9 11.7 %cholesky.231 = f32[128,128]{1,0:T(8,128)S(1)} custom-call(f32[128,128]{1,0:T(8,128)S(1)} %convolution_subtract_fusion.7), custom_call_target="Cholesky" | custom-call | tf_op jit(solution)/shard_map/jit(cholesky)/cholesky | solution.py:52
  330.7 4.5 while.8
  331.9 1.4 bitcast_dynamic-update-slice_fusion.8
  333.8 1.4 bitcast_dynamic-update-slice_fusion.8
  335.2 19.7 %custom-call.18 = f32[2,128,128]{1,2,0:T(8,128)S(1)} custom-call(f32[2,128,128]{2,1,0:T(8,128)S(1)} %get-tuple-element.33), custom_call_target="InvertDiagBlocksLowerTriangular" | custom-call | tf_op jit(solution)/shard_map/triangular_solve/custom-call.0 | solution.py:53
  357.3 45.1 %all-gather.7.cloned.1.call-done = f32[2048,256]{0,1:T(8,128)} async-done(((f32[512,256]{0,1:T(8,128)}), f32[2048,256]{0,1:T(8,128)}) %all-gather.7.cloned.1.call-update) | async-done | bytes 2097168 | tf_op jit(solution)/shard_map/all_gather | solution.py:33
  402.3 6.1 fusion.13
  408.4 1.7 fusion.76
  410.4 34.3 %all-reduce.14.cloned.1.call-done = f32[256,256]{0,1:T(8,128)} async-done(((f32[256,256]{0,1:T(8,128)}), f32[256,256]{0,1:T(8,128)}) %all-reduce.14.cloned.1.call-update) | async-done | bytes 262160 | tf_op jit(solution)/shard_map/psum | solution.py:97
  446.7 11.7 %cholesky.248 = f32[128,128]{1,0:T(8,128)S(1)} custom-call(f32[128,128]{1,0:T(8,128)S(1)} %cholesky.349), custom_call_target="Cholesky" | custom-call | tf_op jit(solution)/shard_map/jit(cholesky)/cholesky | solution.py:52
  458.5 9.8 %custom-call.19 = f32[1,128,128]{1,2,0:T(8,128)S(1)} custom-call(f32[1,128,128]{2,1,0:T(8,128)S(1)} %get-tuple-element.90), custom_call_target="InvertDiagBlocksLowerTriangular" | custom-call | tf_op jit(solution)/shard_map/jit(cholesky)/cholesky | solution.py:52
  468.8 11.7 %cholesky.265 = f32[128,128]{1,0:T(8,128)S(1)} custom-call(f32[128,128]{1,0:T(8,128)S(1)} %convolution_subtract_fusion.6), custom_call_target="Cholesky" | custom-call | tf_op jit(solution)/shard_map/jit(cholesky)/cholesky | solution.py:52
  483.2 4.2 while.9
  487.3 19.7 %custom-call.20 = f32[2,128,128]{1,2,0:T(8,128)S(1)} custom-call(f32[2,128,128]{2,1,0:T(8,128)S(1)} %get-tuple-element.34), custom_call_target="InvertDiagBlocksLowerTriangular" | custom-call | tf_op jit(solution)/shard_map/triangular_solve/custom-call.0 | solution.py:53
  509.4 45.1 %all-gather.9.cloned.1.call-done = f32[2048,256]{0,1:T(8,128)} async-done(((f32[512,256]{0,1:T(8,128)}), f32[2048,256]{0,1:T(8,128)}) %all-gather.9.cloned.1.call-update) | async-done | bytes 2097168 | tf_op jit(solution)/shard_map/all_gather | solution.py:33
  554.5 6.1 fusion.11
  560.5 1.7 fusion.77
  562.6 34.1 %all-reduce.16.cloned.1.call-done = f32[256,256]{0,1:T(8,128)} async-done(((f32[256,256]{0,1:T(8,128)}), f32[256,256]{0,1:T(8,128)}) %all-reduce.16.cloned.1.call-update) | async-done | bytes 262160 | tf_op jit(solution)/shard_map/psum | solution.py:97
  598.8 11.7 %cholesky.282 = f32[128,128]{1,0:T(8,128)S(1)} custom-call(f32[128,128]{1,0:T(8,128)S(1)} %cholesky.352), custom_call_target="Cholesky" | custom-call | tf_op jit(solution)/shard_map/jit(cholesky)/cholesky | solution.py:52
  610.6 9.8 %custom-call.21 = f32[1,128,128]{1,2,0:T(8,128)S(1)} custom-call(f32[1,128,128]{2,1,0:T(8,128)S(1)} %get-tuple-element.86), custom_call_target="InvertDiagBlocksLowerTriangular" | custom-call | tf_op jit(solution)/shard_map/jit(cholesky)/cholesky | solution.py:52
  620.9 11.7 %cholesky.299 = f32[128,128]{1,0:T(8,128)S(1)} custom-call(f32[128,128]{1,0:T(8,128)S(1)} %convolution_subtract_fusion.5), custom_call_target="Cholesky" | custom-call | tf_op jit(solution)/shard_map/jit(cholesky)/cholesky | solution.py:52
  635.3 15.9 %while.10 = (s32[]{:T(128)}, f32[256,256]{1,0:T(8,128)S(1)}, s32[2,2]{1,0:T(2,128)S(1)}, f32[2,128,128]{2,1,0:T(8,128)S(1)}, s32[]{:T(128)}) while((s32[]{:T(128)}, f32[256,256]{1,0:T(8,128)S(1)}, s32[2,2]{1,0:T(2,128)S(1)}, f32[2,128,128]{2,1,0:T(8,128)S(1)}, s32[]{:T(128)}) %tuple.114), condition=%wide.while_cond.clone.1, body=%wide.while_body.clone.1.sunk | while | flops 2 | bytes 131181 | solution.py:53
  647.8 1.4 bitcast_dynamic-update-slice_fusion.10
  651.2 19.7 %custom-call.22 = f32[2,128,128]{1,2,0:T(8,128)S(1)} custom-call(f32[2,128,128]{2,1,0:T(8,128)S(1)} %get-tuple-element.35), custom_call_target="InvertDiagBlocksLowerTriangular" | custom-call | tf_op jit(solution)/shard_map/triangular_solve/custom-call.0 | solution.py:53
  673.2 45.1 %all-gather.11.cloned.1.call-done = f32[2048,256]{0,1:T(8,128)} async-done(((f32[512,256]{0,1:T(8,128)}), f32[2048,256]{0,1:T(8,128)}) %all-gather.11.cloned.1.call-update) | async-done | bytes 2097168 | tf_op jit(solution)/shard_map/all_gather | solution.py:33
  718.3 6.1 fusion.9
  724.4 1.7 fusion.78
  726.1 34.5 %all-reduce.18.cloned.1.call-done = f32[256,256]{0,1:T(8,128)} async-done(((f32[256,256]{0,1:T(8,128)}), f32[256,256]{0,1:T(8,128)}) %all-reduce.18.cloned.1.call-update) | async-done | bytes 262160 | tf_op jit(solution)/shard_map/psum | solution.py:97
  762.7 11.7 %cholesky.316 = f32[128,128]{1,0:T(8,128)S(1)} custom-call(f32[128,128]{1,0:T(8,128)S(1)} %cholesky.355), custom_call_target="Cholesky" | custom-call | tf_op jit(solution)/shard_map/jit(cholesky)/cholesky | solution.py:52
  774.5 9.8 %custom-call.23 = f32[1,128,128]{1,2,0:T(8,128)S(1)} custom-call(f32[1,128,128]{2,1,0:T(8,128)S(1)} %get-tuple-element.82), custom_call_target="InvertDiagBlocksLowerTriangular" | custom-call | tf_op jit(solution)/shard_map/jit(cholesky)/cholesky | solution.py:52
  784.8 11.7 %cholesky.333 = f32[128,128]{1,0:T(8,128)S(1)} custom-call(f32[128,128]{1,0:T(8,128)S(1)} %convolution_subtract_fusion.4), custom_call_target="Cholesky" | custom-call | tf_op jit(solution)/shard_map/jit(cholesky)/cholesky | solution.py:52
  799.3 4.1 while.11
  799.9 1.4 bitcast_dynamic-update-slice_fusion.11
  801.9 1.4 bitcast_dynamic-update-slice_fusion.11
  803.4 19.9 %custom-call.24 = f32[2,128,128]{1,2,0:T(8,128)S(1)} custom-call(f32[2,128,128]{2,1,0:T(8,128)S(1)} %get-tuple-element.36), custom_call_target="InvertDiagBlocksLowerTriangular" | custom-call | tf_op jit(solution)/shard_map/triangular_solve/custom-call.0 | solution.py:53
  (126 shorter events, 37.0 us)
Async XLA Ops:
  7.4 25.3 %reduce-scatter.2.cloned.1.call-start = ((), (), s32[]{:S(2)}) async-start(), calls=%async_computation.1 | async-start | bytes 786432 | tf_op jit(solution)/shard_map/reduce_scatter | solution.py:67
  15.2 9.1 %copy-start = (s32[1,128]{1,0:T(1,128)S(1)}, s32[1,128]{1,0:T(1,128)}, u32[]{:S(2)}) copy-start(s32[1,128]{1,0:T(1,128)} %param.13) | copy-start | bytes 1540
  15.2 123.5 %all-reduce.8.cloned.1.call-start = ((), (), s32[]{:S(2)}) async-start(), calls=%async_computation.2 | async-start | bytes 8388608 | tf_op jit(solution)/shard_map/psum | solution.py:88
  52.2 86.6 %all-gather.5.cloned.1.call-start = ((), (), s32[]{:S(2)}) async-start(), calls=%async_computation.4 | async-start | bytes 2621440 | tf_op jit(solution)/shard_map/all_gather | solution.py:33
  52.8 196.4 %all-reduce.10.cloned.1.call-start = ((), (), s32[]{:S(2)}) async-start(), calls=%async_computation.3 | async-start | bytes 8388608 | tf_op jit(solution)/shard_map/psum | solution.py:88
  138.7 154.0 %all-reduce.12.cloned.1.call-start = ((), (), s32[]{:S(2)}) async-start(), calls=%async_computation.5 | async-start | bytes 524288 | tf_op jit(solution)/shard_map/psum | solution.py:97
  257.1 145.3 %all-gather.7.cloned.1.call-start = ((), (), s32[]{:S(2)}) async-start(), calls=%async_computation.6 | async-start | bytes 2621440 | tf_op jit(solution)/shard_map/all_gather | solution.py:33
  357.2 87.4 %all-reduce.14.cloned.1.call-start = ((), (), s32[]{:S(2)}) async-start(), calls=%async_computation.7 | async-start | bytes 524288 | tf_op jit(solution)/shard_map/psum | solution.py:97
  410.1 144.3 %all-gather.9.cloned.1.call-start = ((), (), s32[]{:S(2)}) async-start(), calls=%async_computation.8 | async-start | bytes 2621440 | tf_op jit(solution)/shard_map/all_gather | solution.py:33
  509.3 87.4 %all-reduce.16.cloned.1.call-start = ((), (), s32[]{:S(2)}) async-start(), calls=%async_computation.9 | async-start | bytes 524288 | tf_op jit(solution)/shard_map/psum | solution.py:97
  562.3 156.0 %all-gather.11.cloned.1.call-start = ((), (), s32[]{:S(2)}) async-start(), calls=%async_computation.10 | async-start | bytes 2621440 | tf_op jit(solution)/shard_map/all_gather | solution.py:33
  673.1 87.4 %all-reduce.18.cloned.1.call-start = ((), (), s32[]{:S(2)}) async-start(), calls=%async_computation.11 | async-start | bytes 524288 | tf_op jit(solution)/shard_map/psum | solution.py:97
Sparse Core Ops, SparseCore 0:
  15.3 17.3 reduce-scatter.1
  52.4 86.2 all-reduce.7
  141.1 108.0 all-reduce.9
Sparse Core Ops, SparseCore 1:
  54.3 46.3 all-gather.4
  257.2 35.5 all-reduce.11
  357.3 45.0 all-gather.6
  410.2 34.3 all-reduce.13
  509.4 45.0 all-gather.8
  562.3 34.3 all-reduce.15
  673.2 45.0 all-gather.10
  726.2 34.3 all-reduce.17
